TPU v7x, 128 devices: a whole 4x4x4 slice. The times are simulated.
128 devices in a mesh: row: 16 (over x, z), col: 8 (over y, core).
Axes of the slice: x: 4, y: 4, z: 4, core: 2. Of those that a mesh axis runs over, the one named last changes fastest.
Arguments:
- teacher_rows: bfloat16 [256, 8192], P('col', 'row'), may hold values from -6 to 6
- projection: bfloat16 [8192, 4608], P('row'), may hold values from -0.0625 to 0.0625
- student_in: bfloat16 [256, 4608], P('col', 'row'), may hold values from -36 to 36, as said below
- norm_gain: bfloat16 [4608], P('row'), may hold values from 0.5 to 1.5
- w_gate: bfloat16 [4608, 36864], P('row', 'col'), may hold values from -0.09375 to 0.09375
- w_up: bfloat16 [4608, 36864], P('row', 'col'), may hold values from -0.09375 to 0.09375
- w_down: bfloat16 [4608, 36864], P('row', 'col'), may hold values from -0.03125 to 0.03125
- row_old: float32 [3, 4608], P(None, 'row'), may hold values from 1.953125e-05 to 0.001953125
- col_old: float32 [3, 36864], P(None, 'col'), may hold values from 1.953125e-05 to 0.001953125
Outputs:
- update_gate: bfloat16 [4608, 36864], P('row', 'col')
- update_up: bfloat16 [4608, 36864], P('row', 'col')
- update_down: bfloat16 [4608, 36864], P('row', 'col')
- row_factors: float32 [3, 4608], P(None, 'row')
- col_factors: float32 [3, 36864], P(None, 'col')
- distill_loss: float32 [], replicated
Inputs may be any that keep to these rules, and one draw needn't show every extreme that they name: `student_in`: student hidden rows of varying magnitude.
All inputs are finite; a program needn't handle non-finite values.
Results may differ from a plain program's by a relative error of at most 0.0075.
Values may be sent and summed in bfloat16 or wider, within the bound.
A program may use at most 128 MiB of HBM per device.

v0:
```python
import math
import jax
import jax.numpy as jnp
from jax import lax
from jax.sharding import PartitionSpec as P

D = 4608
FF = 36864


def gelu_pair(values):
    root_coef = math.sqrt(2.0 / math.pi)
    tangent = jnp.tanh(root_coef * (values + 0.044715 * values * values * values))
    gelu_val = 0.5 * values * (1.0 + tangent)
    gelu_slope = 0.5 * (1.0 + tangent) + 0.5 * values * (1.0 - tangent * tangent) * root_coef * (
        1.0 + 3.0 * 0.044715 * values * values
    )
    return (gelu_val, gelu_slope)


def shards(teacher_rows, projection, student_in, norm_gain, w_gate, w_up, w_down, row_old, col_old):
    decay_rate = 0.8
    target = lax.psum_scatter(
        lax.dot_general(
            projection, teacher_rows, (((0,), (1,)), ((), ())), preferred_element_type=jnp.float32
        ),
        "row",
        scatter_dimension=0,
        tiled=True,
    ).T.astype(jnp.bfloat16)
    inputs = student_in.astype(jnp.float32)
    mean_sq = lax.psum(jnp.sum(inputs * inputs, axis=1), "row") / D
    inv_rms = (1.0 / jnp.sqrt(mean_sq + 1e-06))[:, None]
    normed = (inputs * inv_rms * norm_gain.astype(jnp.float32)[None, :]).astype(jnp.bfloat16)
    normed_all = lax.all_gather(normed, "col", axis=0, tiled=True)
    tokens_all = normed_all.shape[0]
    gate_part = jnp.dot(normed_all, w_gate, preferred_element_type=jnp.float32)
    up_part = jnp.dot(normed_all, w_up, preferred_element_type=jnp.float32)
    gate_sum, up_sum = lax.psum((gate_part, up_part), "row")
    gelu_val, gelu_slope = gelu_pair(gate_sum)
    hidden = (gelu_val * up_sum).astype(jnp.bfloat16)
    down_out = lax.psum_scatter(
        lax.dot_general(
            hidden, w_down, (((1,), (1,)), ((), ())), preferred_element_type=jnp.float32
        ),
        "col",
        scatter_dimension=0,
        tiled=True,
    )
    residue = inputs + down_out - target.astype(jnp.float32)
    loss_local = jnp.sum(residue * residue)
    loss_raw = lax.psum(loss_local, ("row", "col"))
    grad_out = (residue / tokens_all).astype(jnp.bfloat16)
    grad_all = lax.all_gather(grad_out, "col", axis=0, tiled=True)
    grad_down = lax.dot_general(
        grad_all, hidden, (((0,), (0,)), ((), ())), preferred_element_type=jnp.float32
    )
    hidden_part = jnp.dot(grad_all, w_down, preferred_element_type=jnp.float32)
    grad_hidden = lax.psum(hidden_part, "row")
    grad_gatein = (grad_hidden * up_sum * gelu_slope).astype(jnp.bfloat16)
    grad_upin = (grad_hidden * gelu_val).astype(jnp.bfloat16)
    grad_gate = lax.dot_general(
        normed_all, grad_gatein, (((0,), (0,)), ((), ())), preferred_element_type=jnp.float32
    )
    grad_up = lax.dot_general(
        normed_all, grad_upin, (((0,), (0,)), ((), ())), preferred_element_type=jnp.float32
    )
    gradients = [grad_gate, grad_up, grad_down]
    squares = [gradient * gradient + 1e-30 for gradient in gradients]
    row_sums = lax.psum(
        (jnp.sum(squares[0], axis=1), jnp.sum(squares[1], axis=1), jnp.sum(squares[2], axis=1)),
        "col",
    )
    col_sums = lax.psum(
        (jnp.sum(squares[0], axis=0), jnp.sum(squares[1], axis=0), jnp.sum(squares[2], axis=0)),
        "row",
    )
    row_new = [
        decay_rate * row_old[which] + (1.0 - decay_rate) * row_sums[which] / FF
        for which in range(3)
    ]
    col_new = [
        decay_rate * col_old[which] + (1.0 - decay_rate) * col_sums[which] / D for which in range(3)
    ]
    updates = [
        gradients[which] / jnp.sqrt(row_new[which][:, None] * col_new[which][None, :])
        for which in range(3)
    ]
    update_sums = [jnp.sum(update * update) for update in updates]
    totals = lax.psum((update_sums[0], update_sums[1], update_sums[2]), ("row", "col"))
    clipped = [
        (updates[which] / jnp.maximum(1.0, jnp.sqrt(totals[which] / (D * FF)))).astype(jnp.bfloat16)
        for which in range(3)
    ]
    loss_total = 0.5 * loss_raw / tokens_all
    return (clipped[0], clipped[1], clipped[2], jnp.stack(row_new), jnp.stack(col_new), loss_total)


def solution(mesh):
    placed = (
        P("col", "row"),
        P("row", None),
        P("col", "row"),
        P("row"),
        P("row", "col"),
        P("row", "col"),
        P("row", "col"),
        P(None, "row"),
        P(None, "col"),
    )
    return jax.shard_map(
        shards,
        mesh=mesh,
        in_specs=placed,
        out_specs=(
            P("row", "col"),
            P("row", "col"),
            P("row", "col"),
            P(None, "row"),
            P(None, "col"),
            P(),
        ),
        check_vma=False,
    )
```

profile of v0, /device:TPU:1, one launch (start us, length us, event | category | flops | bytes accessed | tf_op | source)
XLA Modules:
  0.0 661.3 jit_solution(16342523229148362279)
XLA Ops:
  7.2 0.0 copy-start
  7.2 0.0 all-reduce.9.cloned.1.call-start
  7.2 0.8 convert_element_type.41
  8.1 0.8 fusion.16
  8.9 35.4 %psum.98 = f32[32]{0:T(128)S(1)} all-reduce(f32[32]{0:T(128)S(1)} %fusion.16), channel_id=1, replica_groups=mesh['row'=16,'col'=8] {'row'}, use_global_device_ids=true, to_apply=%region_1.0 | all-reduce | flops 32 | bytes 256 | tf_op jit(solution)/shard_map/psum | solution.py:32
  44.3 0.0 copy-start.6
  44.3 1.0 fusion.18
  45.3 20.9 %all_gather.6 = bf16[256,288]{1,0:T(8,128)(2,1)S(1)} all-gather(bf16[32,288]{1,0:T(8,128)(2,1)S(1)} %fusion.18), channel_id=1, replica_groups=mesh['row'=16,'col'=8] {'col'}, dimensions={0}, use_global_device_ids=true | all-gather | bytes 165888 | tf_op jit(solution)/shard_map/all_gather | solution.py:35
  66.2 5.3 fusion.29
  71.5 0.0 copy-done.6
  71.5 3.6 fusion.30
  75.0 0.0 copy-start.9
  75.1 0.0 all-reduce.9.cloned.1.call-update
  75.1 0.0 reduce-scatter.7.cloned.1.call-start
  75.1 0.7 copy-done.9
  75.8 5.7 fusion.33
  81.5 0.0 reduce-scatter.7.cloned.1.call-update
  81.5 0.0 reduce-scatter.5.cloned.1.call-start
  81.6 138.9 %all-reduce.9.cloned.1.call-done = (f32[256,4608]{1,0:T(8,128)}, f32[256,4608]{1,0:T(8,128)}) async-done(((f32[256,4608]{1,0:T(8,128)}, f32[256,4608]{1,0:T(8,128)}), (f32[256,4608]{1,0:T(8,128)}, f32[256,4608]{1,0:T(8,128)})) %all-reduce.9.cloned.1.call-update) | async-done | bytes 9437200 | tf_op jit(solution)/shard_map/psum | solution.py:39
  220.5 4.6 multiply_convert_fusion.1
  225.1 0.0 copy-start.4
  225.1 1.4 copy-done.4
  226.5 0.0 copy-done
  226.5 0.0 copy-start.7
  226.5 2.1 fusion.31
  228.7 0.0 reduce-scatter.5.cloned.1.call-update
  228.7 0.0 all-reduce.7.cloned.1.call-start
  228.7 69.7 %reduce-scatter.7.cloned.1.call-done = f32[288,32]{1,0:T(8,128)} async-done(((f32[4608,32]{1,0:T(8,128)}), f32[288,32]{1,0:T(8,128)}) %reduce-scatter.7.cloned.1.call-update) | async-done | bytes 36880
  298.4 1.0 copy.16
  299.4 31.4 %reduce-scatter.5.cloned.1.call-done = f32[32,288]{1,0:T(8,128)} async-done(((f32[256,288]{1,0:T(8,128)}), f32[32,288]{1,0:T(8,128)}) %reduce-scatter.5.cloned.1.call-update) | async-done | bytes 36880 | tf_op jit(solution)/shard_map/reduce_scatter | solution.py:42
  330.9 0.0 copy-done.7
  330.9 1.4 multiply_reduce_fusion.3
  332.3 16.1 %all_gather.7 = bf16[256,288]{1,0:T(8,128)(2,1)S(1)} all-gather(bf16[32,288]{1,0:T(8,128)(2,1)S(1)} %get-tuple-element.31), channel_id=1, replica_groups=mesh['row'=16,'col'=8] {'col'}, dimensions={0}, use_global_device_ids=true | all-gather | bytes 165888 | tf_op jit(solution)/shard_map/all_gather | solution.py:54
  348.3 0.0 copy-start.10
  348.3 0.0 copy-start.8
  348.3 3.6 fusion.32
  351.9 0.0 copy-start.5
  351.9 0.0 all-reduce.7.cloned.1.call-update
  351.9 0.0 copy-done.10
  352.0 0.0 copy-done.8
  352.0 0.2 multiply_reduce_fusion.4
  352.2 1.4 copy-done.5
  353.6 3.3 fusion.12
  356.9 102.5 %all-reduce.7.cloned.1.call-done = f32[256,4608]{1,0:T(8,128)} async-done(((f32[256,4608]{1,0:T(8,128)}), f32[256,4608]{1,0:T(8,128)}) %all-reduce.7.cloned.1.call-update) | async-done | bytes 4718608 | tf_op jit(solution)/shard_map/psum | solution.py:59
  459.3 0.0 copy-start.11
  459.3 9.0 %fusion.8 = (f32[288]{0:T(512)S(1)}, f32[4608]{0:T(1024)S(1)}, f32[288,4608]{1,0:T(8,128)}) fusion(bf16[256,288]{1,0:T(8,128)(2,1)S(1)} %all_gather.6, f32[256,4608]{1,0:T(8,128)} %get-tuple-element.25, f32[256,4608]{1,0:T(8,128)} %all-reduce.7.cloned.1.call-done, f32[256,4608]{1,0:T(8,128)} %get-tuple-element.26), kind=kOutput, calls=%fused_computation.24 | convolution fusion | flops 708373760 | bytes 19631232 | tf_op jit(solution)/shard_map/dot_general | solution.py:62
  468.3 0.0 copy-done.11
  468.3 7.3 %fusion.10 = (f32[288]{0:T(512)S(1)}, f32[4608]{0:T(1024)S(1)}, f32[288,4608]{1,0:T(8,128)}) fusion(bf16[256,288]{1,0:T(8,128)(2,1)S(1)} %all_gather.6, f32[256,4608]{1,0:T(8,128)S(1)} %copy-done.11, f32[256,4608]{1,0:T(8,128)} %get-tuple-element.25), kind=kOutput, calls=%fused_computation.26 | convolution fusion | flops 696577280 | bytes 14912640 | tf_op jit(solution)/shard_map/dot_general | solution.py:65
  475.7 12.8 %all-reduce.3 = (f32[288]{0:T(512)S(1)}, f32[288]{0:T(512)S(1)}, f32[288]{0:T(512)S(1)}) all-reduce(f32[288]{0:T(512)S(1)} %get-tuple-element.10, f32[288]{0:T(512)S(1)} %get-tuple-element.8, f32[288]{0:T(512)S(1)} %get-tuple-element.6), channel_id=1, replica_groups=mesh['row'=16,'col'=8] {'col'}, use_global_device_ids=true, to_apply=%region_8.0 | all-reduce | flops 864 | bytes 6912 | tf_op jit(solution)/shard_map/psum | solution.py:70
  488.5 58.5 %all-reduce.1 = (f32[4608]{0:T(1024)S(1)}, f32[4608]{0:T(1024)S(1)}, f32[4608]{0:T(1024)S(1)}) all-reduce(f32[4608]{0:T(1024)S(1)} %get-tuple-element.11, f32[4608]{0:T(1024)S(1)} %get-tuple-element.9, f32[4608]{0:T(1024)S(1)} %get-tuple-element.7), channel_id=1, replica_groups=mesh['row'=16,'col'=8] {'row'}, use_global_device_ids=true, to_apply=%region_10.0 | all-reduce | flops 13824 | bytes 110592 | tf_op jit(solution)/shard_map/psum | solution.py:74
  547.0 0.0 copy-start.2
  547.0 4.7 multiply_reduce_fusion.2
  551.7 0.0 copy-done.3
  551.7 2.4 multiply_reduce_fusion.1
  554.1 0.0 copy-done.2
  554.1 2.4 multiply_reduce_fusion
  556.5 78.3 %all-reduce = (f32[]{:T(128)}, f32[]{:T(128)}, f32[]{:T(128)}, f32[]{:T(128)}) all-reduce(f32[]{:T(128)} %multiply_reduce_fusion.2, f32[]{:T(128)} %multiply_reduce_fusion.1, f32[]{:T(128)} %multiply_reduce_fusion, f32[]{:T(128)} %get-tuple-element.30), channel_id=1, replica_groups=mesh['row'=16,'col'=8] {'row','col'}, use_global_device_ids=true, to_apply=%region_12.0 | all-reduce | flops 4 | bytes 32 | tf_op jit(solution)/shard_map/psum | solution.py:90
  635.5 4.9 divide_convert_fusion.2
  641.1 0.0 copy-start.1
  641.1 5.0 divide_convert_fusion.1
  646.8 4.9 divide_convert_fusion
  652.4 0.6 pad_maximum_fusion.1
  653.0 0.7 pad_maximum_fusion
  653.7 0.0 copy-done.1
  (13 shorter events, 0.1 us)
Async XLA Ops:
  7.2 219.3 %copy-start = (bf16[288,4608]{1,0:T(8,128)(2,1)S(1)}, bf16[288,4608]{1,0:T(8,128)(2,1)}, u32[]{:S(2)}) copy-start(bf16[288,4608]{1,0:T(8,128)(2,1)} %param.15) | copy-start | bytes 7962628
  7.2 213.3 %all-reduce.9.cloned.1.call-start = ((), (), s32[]{:S(2)}) async-start(), calls=%async_computation.5 | async-start | bytes 18874368 | tf_op jit(solution)/shard_map/psum | solution.py:39
  44.3 27.2 %copy-start.6 = (bf16[288,4608]{1,0:T(8,128)(2,1)S(1)}, bf16[288,4608]{1,0:T(8,128)(2,1)}, u32[]{:S(2)}) copy-start(bf16[288,4608]{1,0:T(8,128)(2,1)} %param.14) | copy-start | bytes 7962628
  75.0 0.8 copy-start.9
  75.1 223.4 %reduce-scatter.7.cloned.1.call-start = ((), (), s32[]{:S(2)}) async-start(), calls=%async_computation.4 | async-start | bytes 2506752
  81.5 249.3 %reduce-scatter.5.cloned.1.call-start = ((), (), s32[]{:S(2)}) async-start(), calls=%async_computation.2 | async-start | bytes 442368 | tf_op jit(solution)/shard_map/reduce_scatter | solution.py:42
  225.1 1.4 copy-start.4
  226.5 104.3 %copy-start.7 = (bf16[32,288]{1,0:T(8,128)(2,1)S(1)}, bf16[32,288]{1,0:T(8,128)(2,1)}, u32[]{:S(2)}) copy-start(bf16[32,288]{1,0:T(8,128)(2,1)} %param.11) | copy-start | bytes 55300
  228.7 230.7 %all-reduce.7.cloned.1.call-start = ((), (), s32[]{:S(2)}) async-start(), calls=%async_computation.3 | async-start | bytes 9437184 | tf_op jit(solution)/shard_map/psum | solution.py:59
  348.3 3.6 copy-start.10
  348.3 3.6 copy-start.8
  351.9 1.7 copy-start.5
  459.3 9.0 %copy-start.11 = (f32[256,4608]{1,0:T(8,128)S(1)}, f32[256,4608]{1,0:T(8,128)}, u32[]{:S(2)}) copy-start(f32[256,4608]{1,0:T(8,128)} %all-reduce.7.cloned.1.call-done) | copy-start | bytes 14155780
  546.9 4.8 copy-start.3
  547.0 7.2 %copy-start.2 = (f32[288,4608]{1,0:T(8,128)S(1)}, f32[288,4608]{1,0:T(8,128)}, u32[]{:S(2)}) copy-start(f32[288,4608]{1,0:T(8,128)} %get-tuple-element.34) | copy-start | bytes 15925252
  641.1 12.6 %copy-start.1 = (bf16[288,4608]{1,0:T(8,128)(2,1)S(1)}, bf16[288,4608]{1,0:T(8,128)(2,1)}, u32[]{:S(2)}) copy-start(bf16[288,4608]{1,0:T(8,128)(2,1)} %param.15) | copy-start | bytes 7962628
Sparse Core Ops, SparseCore 0:
  75.2 145.2 all-reduce.8
  224.4 74.0 reduce-scatter.6
  301.4 29.4 reduce-scatter.4
  352.1 107.2 all-reduce.6
where the time goes:
time: 662 us; the launch traced here: 661 us
  waiting for transfers between devices  343 us (52%)
  blocking collectives  222 us (34%)
  matrix products  39.8 us (6%)
  other arithmetic  34.5 us (5%)
  between operations  17.8 us (3%)
    psum x1, waiting for transfers between devices, shards(): gate_sum, up_sum = lax.psum((gate_part, up_part), 'row')  139 us
    psum x1, waiting for transfers between devices, shards(): grad_hidden = lax.psum(hidden_part, 'row')  102 us
    psum x1, blocking collectives, shards(): lax.psum((update_sums[0], update_sums[1], update_sums[2]), ('row', 'col'))  78.3 us
    unnamed x5, waiting for transfers between devices  69.8 us
    psum x1, blocking collectives, shards(): lax.psum((jnp.sum(squares[0], axis=0), jnp.sum(squares[1], axis=0), jnp.s...  58.5 us
    psum x1, blocking collectives, shards(): mean_sq = lax.psum(jnp.sum(inputs * inputs, axis=1), 'row') / D  35.4 us
    reduce_scatter x1, waiting for transfers between devices, shards(): lax.psum_scatter(lax.dot_general(hidden, w_down, (((1,), (1,)), ((), ()))...  31.4 us
    all_gather x1, blocking collectives, shards(): normed_all = lax.all_gather(normed, 'col', axis=0, tiled=True)  20.9 us
  transfers between devices with their start and end apart: 4, of which 4 were waited for; matrix products, arithmetic and copies ran while one was open for 3% of the time, Pallas kernels for 0%

commit v1 on v0

--- a/solution.py
+++ b/solution.py
@@ -56,7 +56,11 @@
         grad_all, hidden, (((0,), (0,)), ((), ())), preferred_element_type=jnp.float32
     )
     hidden_part = jnp.dot(grad_all, w_down, preferred_element_type=jnp.float32)
-    grad_hidden = lax.psum(hidden_part, "row")
+    grad_hidden = hidden_part
+    for hop in (1, 2, 4, 8):
+        grad_hidden = grad_hidden + lax.ppermute(
+            grad_hidden, "row", [(dev, dev ^ hop) for dev in range(16)]
+        )
     grad_gatein = (grad_hidden * up_sum * gelu_slope).astype(jnp.bfloat16)
     grad_upin = (grad_hidden * gelu_val).astype(jnp.bfloat16)
     grad_gate = lax.dot_general(

time: 662 us -> 962 us (1.45)
  waiting for transfers between devices: 343 us -> 639 us
    ppermute x0 -> x4, waiting for transfers between devices: none -> 399 us  [shards(): lax.ppermute(grad_hidden, 'row', [(dev, dev ^ hop) for dev in range(16)])]
    psum x1 -> x0, waiting for transfers between devices: 102 us -> none  [shards(): grad_hidden = lax.psum(hidden_part, 'row')]
    unnamed x5 -> x4, waiting for transfers between devices: 69.8 us -> 69.8 us
  transfers between devices with their start and end apart: 4 -> 7, of which waited for: 4 -> 7; matrix products, arithmetic and copies ran while one was open for 3% -> 2% of each run, Pallas kernels for 0% -> 0%
where the time goes in v1:
time: 962 us; the launch traced here: 961 us
  waiting for transfers between devices  639 us (66%)
  blocking collectives  225 us (23%)
  other arithmetic  36.1 us (4%)
  matrix products  31.5 us (3%)
  between operations  17.8 us (2%)
    ppermute x4, waiting for transfers between devices, shards(): lax.ppermute(grad_hidden, 'row', [(dev, dev ^ hop) for dev in range(16)])  399 us
    psum x1, waiting for transfers between devices, shards(): gate_sum, up_sum = lax.psum((gate_part, up_part), 'row')  139 us
    psum x1, blocking collectives, shards(): lax.psum((update_sums[0], update_sums[1], update_sums[2]), ('row', 'col'))  76.6 us
    unnamed x4, waiting for transfers between devices  69.8 us
    psum x1, blocking collectives, shards(): lax.psum((jnp.sum(squares[0], axis=0), jnp.sum(squares[1], axis=0), jnp.s...  60.4 us
    psum x1, blocking collectives, shards(): mean_sq = lax.psum(jnp.sum(inputs * inputs, axis=1), 'row') / D  35.4 us
    reduce_scatter x1, waiting for transfers between devices, shards(): lax.psum_scatter(lax.dot_general(hidden, w_down, (((1,), (1,)), ((), ()))...  31.4 us
    all_gather x1, blocking collectives, shards(): normed_all = lax.all_gather(normed, 'col', axis=0, tiled=True)  20.9 us
  transfers between devices with their start and end apart: 7, of which 7 were waited for; matrix products, arithmetic and copies ran while one was open for 2% of the time, Pallas kernels for 0%

profile of v1, /device:TPU:1, one launch (start us, length us, event | category | flops | bytes accessed | tf_op | source)
XLA Modules:
  0.0 961.3 jit_solution(4182792174013705139)
XLA Ops:
  7.2 0.0 copy-start
  7.2 0.0 all-reduce.6.cloned.1.call-start
  7.2 0.8 convert_element_type.41
  8.1 0.8 fusion.18
  8.9 35.4 %psum.91 = f32[32]{0:T(128)S(1)} all-reduce(f32[32]{0:T(128)S(1)} %fusion.18), channel_id=1, replica_groups=mesh['row'=16,'col'=8] {'row'}, use_global_device_ids=true, to_apply=%region_1.0 | all-reduce | flops 32 | bytes 256 | tf_op jit(solution)/shard_map/psum | solution.py:32
  44.3 1.0 fusion.20
  45.3 20.9 %all_gather.6 = bf16[256,288]{1,0:T(8,128)(2,1)S(1)} all-gather(bf16[32,288]{1,0:T(8,128)(2,1)S(1)} %fusion.20), channel_id=1, replica_groups=mesh['row'=16,'col'=8] {'col'}, dimensions={0}, use_global_device_ids=true | all-gather | bytes 165888 | tf_op jit(solution)/shard_map/all_gather | solution.py:35
  66.2 5.3 fusion.31
  71.5 0.0 copy-done.6
  71.5 3.5 fusion.32
  75.0 0.0 all-reduce.6.cloned.1.call-update
  75.0 0.0 reduce-scatter.7.cloned.1.call-start
  75.1 0.7 copy-done.9
  75.8 5.7 fusion.35
  81.5 0.0 reduce-scatter.7.cloned.1.call-update
  81.5 0.0 reduce-scatter.5.cloned.1.call-start
  81.5 138.9 %all-reduce.6.cloned.1.call-done = (f32[256,4608]{1,0:T(8,128)}, f32[256,4608]{1,0:T(8,128)}) async-done(((f32[256,4608]{1,0:T(8,128)}, f32[256,4608]{1,0:T(8,128)}), (f32[256,4608]{1,0:T(8,128)}, f32[256,4608]{1,0:T(8,128)})) %all-reduce.6.cloned.1.call-update) | async-done | bytes 9437200 | tf_op jit(solution)/shard_map/psum | solution.py:39
  220.5 4.6 multiply_convert_fusion.1
  225.1 0.0 copy-start.4
  225.1 1.4 copy-done.4
  226.5 0.0 copy-done
  226.5 2.1 fusion.33
  228.6 0.0 reduce-scatter.5.cloned.1.call-update
  228.6 69.8 %reduce-scatter.7.cloned.1.call-done = f32[288,32]{1,0:T(8,128)} async-done(((f32[4608,32]{1,0:T(8,128)}), f32[288,32]{1,0:T(8,128)}) %reduce-scatter.7.cloned.1.call-update) | async-done | bytes 36880
  298.4 1.0 copy.16
  299.4 31.4 %reduce-scatter.5.cloned.1.call-done = f32[32,288]{1,0:T(8,128)} async-done(((f32[256,288]{1,0:T(8,128)}), f32[32,288]{1,0:T(8,128)}) %reduce-scatter.5.cloned.1.call-update) | async-done | bytes 36880 | tf_op jit(solution)/shard_map/reduce_scatter | solution.py:42
  330.8 0.0 copy-done.7
  330.8 1.4 multiply_reduce_fusion.3
  332.2 15.9 %all_gather.7 = bf16[256,288]{1,0:T(8,128)(2,1)S(1)} all-gather(bf16[32,288]{1,0:T(8,128)(2,1)S(1)} %get-tuple-element.31), channel_id=1, replica_groups=mesh['row'=16,'col'=8] {'col'}, dimensions={0}, use_global_device_ids=true | all-gather | bytes 165888 | tf_op jit(solution)/shard_map/all_gather | solution.py:54
  348.1 1.4 fusion.34
  349.5 1.3 collective-permute-start
  350.8 102.0 %collective-permute-done = f32[256,4608]{1,0:T(8,128)S(1)} collective-permute-done((f32[256,4608]{1,0:T(8,128)S(1)}, f32[256,4608]{1,0:T(8,128)S(1)}, u32[]{:S(2)}, u32[]{:S(2)}) %collective-permute-start) | collective-permute-done | bytes 4718624 | tf_op jit(solution)/shard_map/ppermute | solution.py:61
  452.8 0.5 add.96
  453.3 2.9 collective-permute-start.1
  456.3 101.0 %collective-permute-done.1 = f32[256,4608]{1,0:T(8,128)S(1)} collective-permute-done((f32[256,4608]{1,0:T(8,128)S(1)}, f32[256,4608]{1,0:T(8,128)S(1)}, u32[]{:S(2)}, u32[]{:S(2)}) %collective-permute-start.1) | collective-permute-done | bytes 4718624 | tf_op jit(solution)/shard_map/ppermute | solution.py:61
  557.3 0.5 add.97
  557.8 0.0 copy-start.10
  557.8 0.0 copy-start.8
  557.8 0.0 copy-start.5
  557.8 0.0 slice-start.1
  557.8 0.0 slice-start.3
  557.9 1.3 collective-permute-start.2
  559.1 100.3 %collective-permute-done.2 = f32[256,4608]{1,0:T(8,128)S(1)} collective-permute-done((f32[256,4608]{1,0:T(8,128)S(1)}, f32[256,4608]{1,0:T(8,128)S(1)}, u32[]{:S(2)}, u32[]{:S(2)}) %collective-permute-start.2) | collective-permute-done | bytes 4718624 | tf_op jit(solution)/shard_map/ppermute | solution.py:61
  659.4 0.5 add.98
  660.0 2.9 collective-permute-start.3
  662.8 0.0 copy-done.10
  662.9 0.2 multiply_reduce_fusion.4
  663.0 3.3 fusion.12
  666.3 96.0 %collective-permute-done.3 = f32[256,4608]{1,0:T(8,128)S(1)} collective-permute-done((f32[256,4608]{1,0:T(8,128)S(1)}, f32[256,4608]{1,0:T(8,128)S(1)}, u32[]{:S(2)}, u32[]{:S(2)}) %collective-permute-start.3) | collective-permute-done | bytes 4718624 | tf_op jit(solution)/shard_map/ppermute | solution.py:61
  762.4 0.0 slice-done
  762.4 5.7 fusion.8
  768.1 4.4 fusion.10
  772.6 15.5 %all-reduce.3 = (f32[288]{0:T(512)S(1)}, f32[288]{0:T(512)S(1)}, f32[288]{0:T(512)S(1)}) all-reduce(f32[288]{0:T(512)S(1)} %get-tuple-element.10, f32[288]{0:T(512)S(1)} %get-tuple-element.8, f32[288]{0:T(512)S(1)} %get-tuple-element.6), channel_id=1, replica_groups=mesh['row'=16,'col'=8] {'col'}, use_global_device_ids=true, to_apply=%region_7.0 | all-reduce | flops 864 | bytes 6912 | tf_op jit(solution)/shard_map/psum | solution.py:74
  788.1 60.4 %all-reduce.1 = (f32[4608]{0:T(1024)S(1)}, f32[4608]{0:T(1024)S(1)}, f32[4608]{0:T(1024)S(1)}) all-reduce(f32[4608]{0:T(1024)S(1)} %get-tuple-element.11, f32[4608]{0:T(1024)S(1)} %get-tuple-element.9, f32[4608]{0:T(1024)S(1)} %get-tuple-element.7), channel_id=1, replica_groups=mesh['row'=16,'col'=8] {'row'}, use_global_device_ids=true, to_apply=%region_9.0 | all-reduce | flops 13824 | bytes 110592 | tf_op jit(solution)/shard_map/psum | solution.py:78
  848.5 4.7 multiply_reduce_fusion.2
  853.3 2.4 multiply_reduce_fusion.1
  855.7 2.4 multiply_reduce_fusion
  858.1 76.6 %all-reduce = (f32[]{:T(128)}, f32[]{:T(128)}, f32[]{:T(128)}, f32[]{:T(128)}) all-reduce(f32[]{:T(128)} %multiply_reduce_fusion.2, f32[]{:T(128)} %multiply_reduce_fusion.1, f32[]{:T(128)} %multiply_reduce_fusion, f32[]{:T(128)} %get-tuple-element.30), channel_id=1, replica_groups=mesh['row'=16,'col'=8] {'row','col'}, use_global_device_ids=true, to_apply=%region_11.0 | all-reduce | flops 4 | bytes 32 | tf_op jit(solution)/shard_map/psum | solution.py:94
  935.4 4.9 divide_convert_fusion.2
  941.0 0.0 copy-start.1
  941.0 5.0 divide_convert_fusion.1
  946.8 4.9 divide_convert_fusion
  952.3 0.6 pad_maximum_fusion.1
  952.9 0.7 pad_maximum_fusion
  (29 shorter events, 0.1 us)
Async XLA Ops:
  7.2 219.3 %copy-start = (bf16[288,4608]{1,0:T(8,128)(2,1)S(1)}, bf16[288,4608]{1,0:T(8,128)(2,1)}, u32[]{:S(2)}) copy-start(bf16[288,4608]{1,0:T(8,128)(2,1)} %param.15) | copy-start | bytes 7962628
  7.2 213.3 %all-reduce.6.cloned.1.call-start = ((), (), s32[]{:S(2)}) async-start(), calls=%async_computation.4 | async-start | bytes 18874368 | tf_op jit(solution)/shard_map/psum | solution.py:39
  44.3 27.2 %copy-start.6 = (bf16[288,4608]{1,0:T(8,128)(2,1)S(1)}, bf16[288,4608]{1,0:T(8,128)(2,1)}, u32[]{:S(2)}) copy-start(bf16[288,4608]{1,0:T(8,128)(2,1)} %param.14) | copy-start | bytes 7962628
  75.0 0.8 copy-start.9
  75.0 223.4 %reduce-scatter.7.cloned.1.call-start = ((), (), s32[]{:S(2)}) async-start(), calls=%async_computation.3 | async-start | bytes 2506752
  81.5 249.3 %reduce-scatter.5.cloned.1.call-start = ((), (), s32[]{:S(2)}) async-start(), calls=%async_computation.2 | async-start | bytes 442368 | tf_op jit(solution)/shard_map/reduce_scatter | solution.py:42
  225.1 1.4 copy-start.4
  226.5 104.3 %copy-start.7 = (bf16[32,288]{1,0:T(8,128)(2,1)S(1)}, bf16[32,288]{1,0:T(8,128)(2,1)}, u32[]{:S(2)}) copy-start(bf16[32,288]{1,0:T(8,128)(2,1)} %param.11) | copy-start | bytes 55300
  349.5 103.3 %collective-permute-start = (f32[256,4608]{1,0:T(8,128)S(1)}, f32[256,4608]{1,0:T(8,128)S(1)}, u32[]{:S(2)}, u32[]{:S(2)}) collective-permute-start(f32[256,4608]{1,0:T(8,128)S(1)} %fusion.34), channel_id=1, source_target_pairs={{0,8},{8,0},{16,24},{24,16},{32,40},{40,32},{48,56},{56,48},{64,72... | collective-permute-start | bytes 14155784 | tf_op jit(solution)/shard_map/ppermute | solution.py:61
  453.3 103.9 %collective-permute-start.1 = (f32[256,4608]{1,0:T(8,128)S(1)}, f32[256,4608]{1,0:T(8,128)S(1)}, u32[]{:S(2)}, u32[]{:S(2)}) collective-permute-start(f32[256,4608]{1,0:T(8,128)S(1)} %add.96), channel_id=1, source_target_pairs={{0,16},{8,24},{16,0},{24,8},{32,48},{40,56},{48,32},{56,40},{64,80... | collective-permute-start | bytes 14155784 | tf_op jit(solution)/shard_map/ppermute | solution.py:61
  557.3 205.1 %slice-start = ((s8[4718592]{0:T(1024)(128)(4,1)}), s8[4194304]{0:T(1024)(128)(4,1)S(1)}, s32[]{:S(2)}) async-start(s8[4718592]{0:T(1024)(128)(4,1)} %bitcast.21), calls=%async_computation.5 | async-start | bytes 8388608
  557.3 205.1 %slice-start.2 = ((s8[4718592]{0:T(1024)(128)(4,1)}), s8[4194304]{0:T(1024)(128)(4,1)S(1)}, s32[]{:S(2)}) async-start(s8[4718592]{0:T(1024)(128)(4,1)} %bitcast.23), calls=%async_computation.7 | async-start | bytes 8388608
  557.8 105.0 %copy-start.10 = (f32[3,288]{1,0:T(4,128)S(1)}, f32[3,288]{1,0:T(4,128)}, u32[]{:S(2)}) copy-start(f32[3,288]{1,0:T(4,128)} %param.16) | copy-start | bytes 10372
  557.8 105.0 %copy-start.8 = (f32[3,4608]{1,0:T(4,128)S(1)}, f32[3,4608]{1,0:T(4,128)}, u32[]{:S(2)}) copy-start(f32[3,4608]{1,0:T(4,128)} %param.17) | copy-start | bytes 165892
  557.8 105.2 %copy-start.5 = (bf16[256,4608]{1,0:T(8,128)(2,1)S(1)}, bf16[256,4608]{1,0:T(8,128)(2,1)}, u32[]{:S(2)}) copy-start(bf16[256,4608]{1,0:T(8,128)(2,1)} %copy-done.4) | copy-start | bytes 7077892
  557.8 204.5 %slice-start.1 = ((s8[4718592]{0:T(1024)(128)(4,1)}), s8[524288]{0:T(1024)(128)(4,1)S(1)}, s32[]{:S(2)}) async-start(s8[4718592]{0:T(1024)(128)(4,1)} %bitcast.21), calls=%async_computation.6 | async-start | bytes 1048576
  557.8 204.5 %slice-start.3 = ((s8[4718592]{0:T(1024)(128)(4,1)}), s8[524288]{0:T(1024)(128)(4,1)S(1)}, s32[]{:S(2)}) async-start(s8[4718592]{0:T(1024)(128)(4,1)} %bitcast.23), calls=%async_computation.8 | async-start | bytes 1048576
  557.9 101.6 %collective-permute-start.2 = (f32[256,4608]{1,0:T(8,128)S(1)}, f32[256,4608]{1,0:T(8,128)S(1)}, u32[]{:S(2)}, u32[]{:S(2)}) collective-permute-start(f32[256,4608]{1,0:T(8,128)S(1)} %add.97), channel_id=1, source_target_pairs={{0,32},{8,40},{16,48},{24,56},{32,0},{40,8},{48,16},{56,24},{64,96... | collective-permute-start | bytes 14155784 | tf_op jit(solution)/shard_map/ppermute | solution.py:61
  660.0 102.4 %collective-permute-start.3 = (f32[256,4608]{1,0:T(8,128)S(1)}, f32[256,4608]{1,0:T(8,128)S(1)}, u32[]{:S(2)}, u32[]{:S(2)}) collective-permute-start(f32[256,4608]{1,0:T(8,128)S(1)} %add.98), channel_id=1, source_target_pairs={{0,64},{8,72},{16,80},{24,88},{32,96},{40,104},{48,112},{56,120},{... | collective-permute-start | bytes 14155784 | tf_op jit(solution)/shard_map/ppermute | solution.py:61
  848.5 4.8 copy-start.3
  848.5 7.2 copy-start.2
  941.0 12.6 %copy-start.1 = (bf16[288,4608]{1,0:T(8,128)(2,1)S(1)}, bf16[288,4608]{1,0:T(8,128)(2,1)}, u32[]{:S(2)}) copy-start(bf16[288,4608]{1,0:T(8,128)(2,1)} %param.15) | copy-start | bytes 7962628
Sparse Core Ops, SparseCore 0:
  75.2 145.2 all-reduce.5
  224.3 74.0 reduce-scatter.6
  301.3 29.4 reduce-scatter.4
